TPU v7x, 512 devices: a whole 4x8x8 slice. The times are simulated.
512 devices in a mesh: chain: 32 (over x_hi, z, core), term: 16 (over y, x_lo).
Axes of the slice: x: 4 (x_hi: 2, x_lo: 2; x = x_hi * 2 + x_lo), y: 8, z: 8, core: 2. Of those that a mesh axis runs over, the one named last changes fastest.
Arguments:
- wavefunction: bfloat16 [32, 4, 256, 256], P('chain')
- left_ops: bfloat16 [32, 128, 256, 256], P('chain', 'term')
- right_ops: bfloat16 [32, 128, 256, 256], P('chain', 'term')
- term_table: int32 [4, 32, 512], P(None, 'chain', 'term'), may hold values from 0 to 7, as said below
- coefficients: float32 [32, 512], P('chain', 'term'), may hold values from -0.1 to 0.3
- term_counts: int32 [32, 16], P('chain', 'term'), may hold values from 1 to 32, as said below
Outputs:
- first_hamiltonian_image: bfloat16 [32, 4, 256, 256], P('chain', None, 'term')
- second_image: bfloat16 [32, 4, 256, 256], P('chain', None, 'term')
Inputs may be any that keep to these rules, and one draw needn't show every extreme that they name: `term_table`: row 0 and 1 (source and target block) lie in 0 to 3, rows 2 and 3 (operator indices) in 0 to 7. `term_counts`: in every bond at least one term device has all 32 slots live.
All inputs are finite; a program needn't handle non-finite values.
Results may differ from a plain program's by a relative error of at most 0.014.
Values may be sent and summed in bfloat16 or wider, within the bound.
No kernel may reach another device: no remote copies, remote signals or barrier semaphores. Data moves between devices by JAX's collectives and lax.ppermute only.
A program may use at most 64 MiB of HBM per device.

v0:
```python
import jax
import jax.numpy as jnp
from jax import lax
from jax.sharding import PartitionSpec as P

epsilon = 1e-06


def shifted(value, axis, steps):
    count = lax.axis_size(axis)
    pairs = [(source, (source + steps) % count) for source in range(count)]
    return lax.ppermute(value, axis, pairs)


def apply_terms(blocks, left_blocks, right_blocks, term_rows, coef_rows, live_count):
    block_count = blocks.shape[0]
    slot_count = term_rows.shape[1]
    source = term_rows[0]
    target = term_rows[1]
    left_selection = left_blocks[term_rows[2]]
    right_selection = right_blocks[term_rows[3]]
    selected_blocks = blocks[source]
    inner_contraction = jnp.einsum(
        "skh,shu->sku", left_selection, selected_blocks, preferred_element_type=jnp.float32
    ).astype(jnp.bfloat16)
    outer_contraction = jnp.einsum(
        "lbe,leu->lbu", inner_contraction, right_selection, preferred_element_type=jnp.float32
    )
    live_mask = jnp.arange(slot_count, dtype=jnp.int32) < live_count
    weights = jnp.where(live_mask, coef_rows, jnp.float32(0.0))
    routing = (target[None, :] == jnp.arange(block_count, dtype=jnp.int32)[:, None]).astype(
        jnp.float32
    ) * weights[None, :]
    return jnp.einsum("kt,tad->kad", routing, outer_contraction, precision=lax.Precision.HIGHEST)


def body(wavefunction, left_ops, right_ops, term_table, coefficients, term_counts):
    blocks = wavefunction[0]
    neighbour = shifted(right_ops, "chain", -1)
    term_rows = term_table[:, 0, :]
    coef_rows = coefficients[0]
    live_count = term_counts[0, 0]
    left_blocks = left_ops[0]
    right_blocks = neighbour[0]
    first_part = apply_terms(blocks, left_blocks, right_blocks, term_rows, coef_rows, live_count)
    term_parts = lax.axis_size("term")
    row_count = blocks.shape[1] // term_parts
    starting_row = lax.axis_index("term") * row_count
    entry_count = float(blocks.shape[0] * blocks.shape[1] * blocks.shape[2])
    wave_f32 = blocks.astype(jnp.float32)
    wave_norm = jnp.sum(wave_f32 * wave_f32) / entry_count + epsilon
    first = lax.psum(first_part, "term")
    rayleigh = jnp.sum(wave_f32 * first) / entry_count / wave_norm
    residual = first - rayleigh * wave_f32
    direction = (residual * lax.rsqrt(jnp.sum(residual * residual) / entry_count + epsilon)).astype(
        jnp.bfloat16
    )
    second_part = apply_terms(
        direction, left_blocks, right_blocks, term_rows, coef_rows, live_count
    )
    second = lax.psum(second_part.astype(jnp.bfloat16), "term").astype(jnp.float32)
    first_rows = lax.dynamic_slice_in_dim(first, starting_row, row_count, 1)
    second_rows = lax.dynamic_slice_in_dim(second, starting_row, row_count, 1)
    return (first_rows[None].astype(jnp.bfloat16), second_rows[None].astype(jnp.bfloat16))


def solution(mesh):
    in_specs = (
        P("chain", None, None, None),
        P("chain", "term", None, None),
        P("chain", "term", None, None),
        P(None, "chain", "term"),
        P("chain", "term"),
        P("chain", "term"),
    )
    out_specs = (P("chain", None, "term", None), P("chain", None, "term", None))
    return jax.shard_map(body, mesh=mesh, in_specs=in_specs, out_specs=out_specs, check_vma=False)
```

profile of v0, /device:TPU:2, one launch (start us, length us, event | category | flops | bytes accessed | tf_op | source)
XLA Modules:
  0.0 389.5 jit_solution(7426124249693122728)
XLA Ops:
  7.2 12.1 %collective-permute-start = (bf16[1,8,256,256]{3,2,1,0:T(8,128)(2,1)}, bf16[1,8,256,256]{3,2,1,0:T(8,128)(2,1)S(1)}, u32[]{:S(2)}, u32[]{:S(2)}) collective-permute-start(bf16[1,8,256,256]{3,2,1,0:T(8,128)(2,1)} %param.8), channel_id=1, source_target_pairs={{0,496},{16,0},{32,16},{48,32},{64,48},{80,64},{96,80},{112,96},{1... | collective-permute-start | bytes 3145736 | tf_op jit(solution)/shard_map/ppermute | solution.py:12
  20.0 1.5 copy.33
  21.5 0.7 fusion.32
  22.2 2.7 gather_fusion.1
  25.0 2.8 gather_fusion
  27.7 0.7 slice_bitcast_fusion
  28.4 3.5 collective-permute-done
  31.9 2.8 gather_fusion.2
  34.7 10.2 %fusion.6 = f32[32,256,256]{2,1,0:T(8,128)} fusion(bf16[32,256,256]{2,1,0:T(8,128)(2,1)} %gather_fusion.2, bf16[32,256,256]{2,1,0:T(8,128)(2,1)} %gather_fusion, bf16[32,256,256]{2,1,0:T(8,128)(2,1)} %gather_fusion.1), kind=kOutput, calls=%fused_computation.10 | convolution fusion | flops 2149580800 | bytes 20971520 | tf_op jit(solution)/shard_map/lbe,leu->lbu/dot_general | solution.py:26
  45.0 13.2 %fusion.2 = f32[4,256,256]{2,0,1:T(4,128)} fusion(f32[32,256,256]{2,1,0:T(8,128)} %fusion.6, f32[32]{0:T(128)S(1)} %fusion.30, s32[32]{0:T(128)S(1)} %slice_bitcast_fusion), kind=kOutput, calls=%fused_computation.6 | convolution fusion | flops 100663552 | bytes 9437440 | tf_op jit(solution)/shard_map/kt,tad->kad/dot_general | solution.py:34
  58.2 0.2 all-reduce.5.cloned.1.call-start
  58.4 144.4 %all-reduce.3.cloned.1.call-done = f32[4,256,256]{2,0,1:T(4,128)} async-done(((f32[4,256,256]{2,0,1:T(4,128)}), f32[4,256,256]{2,0,1:T(4,128)}) %all-reduce.3.cloned.1.call-update) | async-done | bytes 1048592 | tf_op jit(solution)/shard_map/psum | solution.py:52
  202.8 2.4 fusion.16
  206.6 2.4 multiply_reduce_fusion
  209.6 1.7 multiply_convert_fusion
  211.4 0.1 copy.13
  211.4 2.7 gather_fusion.3
  214.2 10.2 %fusion.4 = f32[32,256,256]{2,1,0:T(8,128)} fusion(bf16[32,256,256]{2,1,0:T(8,128)(2,1)} %gather_fusion.2, bf16[32,256,256]{2,1,0:T(8,128)(2,1)} %gather_fusion, bf16[32,256,256]{2,1,0:T(8,128)(2,1)} %gather_fusion.3), kind=kOutput, calls=%fused_computation.8 | convolution fusion | flops 2149580800 | bytes 20971520 | tf_op jit(solution)/shard_map/lbe,leu->lbu/dot_general | solution.py:26
  224.4 13.0 %fusion.12 = bf16[4,256,256]{2,0,1:T(4,128)(2,1)} fusion(f32[32,256,256]{2,1,0:T(8,128)} %fusion.4, f32[32]{0:T(128)S(1)} %fusion.30, s32[32]{0:T(128)S(1)} %slice_bitcast_fusion), kind=kOutput, calls=%fused_computation.17 | convolution fusion | flops 100925696 | bytes 8913152 | tf_op jit(solution)/shard_map/kt,tad->kad/dot_general | solution.py:34
  237.4 0.9 fusion.18
  238.3 0.6 copy.14
  238.9 142.4 %all-reduce.5.cloned.1.call-done = bf16[4,256,256]{2,0,1:T(4,128)(2,1)} async-done(((bf16[4,256,256]{2,0,1:T(4,128)(2,1)}), bf16[4,256,256]{2,0,1:T(4,128)(2,1)}) %all-reduce.5.cloned.1.call-update) | async-done | bytes 524304 | tf_op jit(solution)/shard_map/psum | solution.py:61
  381.3 0.8 fusion.19
  382.1 0.6 copy.15
  (13 shorter events, 0.2 us)
Async XLA Ops:
  7.2 17.8 %copy-start = (bf16[1,8,256,256]{3,2,1,0:T(8,128)(2,1)S(1)}, bf16[1,8,256,256]{3,2,1,0:T(8,128)(2,1)}, u32[]{:S(2)}) copy-start(bf16[1,8,256,256]{3,2,1,0:T(8,128)(2,1)} %param.7) | copy-start | bytes 3145732
  7.2 195.6 %all-reduce.3.cloned.1.call-start = ((), (), s32[]{:S(2)}) async-start(), calls=%async_computation | async-start | bytes 2097152 | tf_op jit(solution)/shard_map/psum | solution.py:52
  7.2 24.7 %collective-permute-start = (bf16[1,8,256,256]{3,2,1,0:T(8,128)(2,1)}, bf16[1,8,256,256]{3,2,1,0:T(8,128)(2,1)S(1)}, u32[]{:S(2)}, u32[]{:S(2)}) collective-permute-start(bf16[1,8,256,256]{3,2,1,0:T(8,128)(2,1)} %param.8), channel_id=1, source_target_pairs={{0,496},{16,0},{32,16},{48,32},{64,48},{80,64},{96,80},{112,96},{1... | collective-permute-start | bytes 3145736 | tf_op jit(solution)/shard_map/ppermute | solution.py:12
  24.9 3.4 copy-start.2
  45.0 157.9 %copy-start.1 = (bf16[1,4,256,256]{3,2,1,0:T(8,128)(2,1)S(1)}, bf16[1,4,256,256]{3,2,1,0:T(8,128)(2,1)}, u32[]{:S(2)}) copy-start(bf16[1,4,256,256]{3,2,1,0:T(8,128)(2,1)} %param.6) | copy-start | bytes 1572868
  58.2 323.1 %all-reduce.5.cloned.1.call-start = ((), (), s32[]{:S(2)}) async-start(), calls=%async_computation.1 | async-start | bytes 1048576 | tf_op jit(solution)/shard_map/psum | solution.py:61
Sparse Core Ops, SparseCore 0:
  58.3 144.4 all-reduce.2
  237.6 143.6 all-reduce.4
where the time goes:
time: 390 us
  waiting for transfers between devices  290 us (74%)
  matrix products  46.7 us (12%)
  between operations  16.8 us (4%)
  local copies, waits for them, and re-layouts  15.4 us (4%)
  starting transfers between devices  12.3 us (3%)
  other arithmetic  7.98 us (2%)
    psum x1, waiting for transfers between devices, body(): first = lax.psum(first_part, 'term')  144 us
    psum x1, waiting for transfers between devices, body(): lax.psum(second_part.astype(jnp.bfloat16), 'term').astype(jnp.float32)  142 us
    dot_general x2, matrix products, apply_terms(): jnp.einsum('kt,tad->kad', routing, outer_contraction, precision=lax.Preci...  26.2 us
    dot_general x2, matrix products, apply_terms(): jnp.einsum('lbe,leu->lbu', inner_contraction, right_selection, preferred_...  20.5 us
    ppermute x1, starting transfers between devices, shifted(): return lax.ppermute(value, axis, pairs)  12.1 us
  transfers between devices with their start and end apart: 3, of which 3 were waited for; matrix products, arithmetic and copies ran while one was open for 3% of the time, Pallas kernels for 0%

commit v1 on v0

--- a/solution.py
+++ b/solution.py
@@ -49,7 +49,7 @@
     entry_count = float(blocks.shape[0] * blocks.shape[1] * blocks.shape[2])
     wave_f32 = blocks.astype(jnp.float32)
     wave_norm = jnp.sum(wave_f32 * wave_f32) / entry_count + epsilon
-    first = lax.psum(first_part, "term")
+    first = jnp.sum(lax.all_gather(first_part, "term"), axis=0)
     rayleigh = jnp.sum(wave_f32 * first) / entry_count / wave_norm
     residual = first - rayleigh * wave_f32
     direction = (residual * lax.rsqrt(jnp.sum(residual * residual) / entry_count + epsilon)).astype(

time: 390 us -> 607 us (1.56)
  waiting for transfers between devices: 290 us -> 506 us
    all_gather x0 -> x1, waiting for transfers between devices: none -> 352 us  [body(): first = jnp.sum(lax.all_gather(first_part, 'term'), axis=0)]
    psum x1 -> x0, waiting for transfers between devices: 144 us -> none  [body(): first = lax.psum(first_part, 'term')]
    psum x1, waiting for transfers between devices: 142 us -> 150 us  [body(): lax.psum(second_part.astype(jnp.bfloat16), 'term').astype(jnp.float32)]
    reduce_sum x0 -> x1, other arithmetic: none -> 7.04 us  [body(): first = jnp.sum(lax.all_gather(first_part, 'term'), axis=0)]
  transfers between devices with their start and end apart: 3 -> 3, of which waited for: 3 -> 3; matrix products, arithmetic and copies ran while one was open for 3% -> 1% of each run, Pallas kernels for 0% -> 0%
where the time goes in v1:
time: 607 us
  waiting for transfers between devices  506 us (83%)
  matrix products  45.8 us (8%)
  between operations  16.8 us (3%)
  local copies, waits for them, and re-layouts  15.4 us (3%)
  starting transfers between devices  12.3 us (2%)
  other arithmetic  10.5 us (2%)
    all_gather x1, waiting for transfers between devices, body(): first = jnp.sum(lax.all_gather(first_part, 'term'), axis=0)  352 us
    psum x1, waiting for transfers between devices, body(): lax.psum(second_part.astype(jnp.bfloat16), 'term').astype(jnp.float32)  150 us
    dot_general x2, matrix products, apply_terms(): jnp.einsum('kt,tad->kad', routing, outer_contraction, precision=lax.Preci...  25.3 us
    dot_general x2, matrix products, apply_terms(): jnp.einsum('lbe,leu->lbu', inner_contraction, right_selection, preferred_...  20.5 us
  transfers between devices with their start and end apart: 3, of which 3 were waited for; matrix products, arithmetic and copies ran while one was open for 1% of the time, Pallas kernels for 0%

profile of v1, /device:TPU:2, one launch (start us, length us, event | category | flops | bytes accessed | tf_op | source)
XLA Modules:
  0.0 607.1 jit_solution(9382430547656041705)
XLA Ops:
  7.2 0.0 all-gather.3.cloned.1.call-start
  7.2 12.1 %collective-permute-start = (bf16[1,8,256,256]{3,2,1,0:T(8,128)(2,1)}, bf16[1,8,256,256]{3,2,1,0:T(8,128)(2,1)S(1)}, u32[]{:S(2)}, u32[]{:S(2)}) collective-permute-start(bf16[1,8,256,256]{3,2,1,0:T(8,128)(2,1)} %param.8), channel_id=1, source_target_pairs={{0,496},{16,0},{32,16},{48,32},{64,48},{80,64},{96,80},{112,96},{1... | collective-permute-start | bytes 3145736 | tf_op jit(solution)/shard_map/ppermute | solution.py:12
  20.0 0.7 fusion.31
  20.7 3.8 gather_fusion.1
  24.5 2.8 gather_fusion
  27.3 0.7 slice_bitcast_fusion
  28.0 4.0 collective-permute-done
  31.9 2.7 gather_fusion.2
  34.7 10.2 %fusion.6 = f32[32,256,256]{2,1,0:T(8,128)} fusion(bf16[32,256,256]{2,1,0:T(8,128)(2,1)} %gather_fusion.2, bf16[32,256,256]{2,1,0:T(8,128)(2,1)} %gather_fusion, bf16[32,256,256]{2,1,0:T(8,128)(2,1)} %gather_fusion.1), kind=kOutput, calls=%fused_computation.10 | convolution fusion | flops 2149580800 | bytes 20971520 | tf_op jit(solution)/shard_map/lbe,leu->lbu/dot_general | solution.py:26
  44.9 12.3 %fusion.2 = f32[4,256,256]{2,0,1:T(4,128)S(1)} fusion(f32[32,256,256]{2,1,0:T(8,128)} %fusion.6, f32[32]{0:T(128)S(1)} %fusion.29, s32[32]{0:T(128)S(1)} %slice_bitcast_fusion), kind=kOutput, calls=%fused_computation.6 | convolution fusion | flops 100663552 | bytes 9437440 | tf_op jit(solution)/shard_map/kt,tad->kad/dot_general | solution.py:34
  57.2 1.3 copy.15
  58.5 0.2 all-reduce.2.cloned.1.call-start
  58.7 352.1 %all-gather.3.cloned.1.call-done = f32[64,256,256]{2,1,0:T(8,128)} async-done(((f32[4,256,256]{2,1,0:T(8,128)}), f32[64,256,256]{2,1,0:T(8,128)}) %all-gather.3.cloned.1.call-update) | async-done | bytes 16777232 | tf_op jit(solution)/shard_map/all_gather | solution.py:52
  410.8 7.0 %reduce_sum.36 = f32[4,256,256]{2,1,0:T(8,128)S(1)} reduce(f32[16,4,256,256]{3,2,1,0:T(8,128)} %bitcast.44, f32[]{:T(128)} %constant.9.clone.1), dimensions={0}, to_apply=%region_0.1 | reduce | flops 3932160 | bytes 17825796 | tf_op jit(solution)/shard_map/reduce_sum | solution.py:52
  417.8 0.9 fusion.16
  420.1 0.9 multiply_reduce_fusion
  421.6 0.2 multiply_convert_fusion
  421.8 2.8 gather_fusion.3
  424.6 10.2 %fusion.4 = f32[32,256,256]{2,1,0:T(8,128)} fusion(bf16[32,256,256]{2,1,0:T(8,128)(2,1)} %gather_fusion.2, bf16[32,256,256]{2,1,0:T(8,128)(2,1)} %gather_fusion, bf16[32,256,256]{2,1,0:T(8,128)(2,1)} %gather_fusion.3), kind=kOutput, calls=%fused_computation.8 | convolution fusion | flops 2149580800 | bytes 20971520 | tf_op jit(solution)/shard_map/lbe,leu->lbu/dot_general | solution.py:26
  434.9 13.0 %fusion.12 = bf16[4,256,256]{2,0,1:T(4,128)(2,1)} fusion(f32[32,256,256]{2,1,0:T(8,128)} %fusion.4, f32[32]{0:T(128)S(1)} %fusion.29, s32[32]{0:T(128)S(1)} %slice_bitcast_fusion), kind=kOutput, calls=%fused_computation.17 | convolution fusion | flops 100925696 | bytes 8913152 | tf_op jit(solution)/shard_map/kt,tad->kad/dot_general | solution.py:34
  447.9 0.6 copy.20
  448.5 150.4 %all-reduce.2.cloned.1.call-done = bf16[4,256,256]{2,0,1:T(4,128)(2,1)} async-done(((bf16[4,256,256]{2,0,1:T(4,128)(2,1)}), bf16[4,256,256]{2,0,1:T(4,128)(2,1)}) %all-reduce.2.cloned.1.call-update) | async-done | bytes 524304 | tf_op jit(solution)/shard_map/psum | solution.py:61
  598.9 0.8 fusion.18
  599.7 0.6 copy.21
  (13 shorter events, 0.1 us)
Async XLA Ops:
  7.2 17.3 %copy-start = (bf16[1,8,256,256]{3,2,1,0:T(8,128)(2,1)S(1)}, bf16[1,8,256,256]{3,2,1,0:T(8,128)(2,1)}, u32[]{:S(2)}) copy-start(bf16[1,8,256,256]{3,2,1,0:T(8,128)(2,1)} %param.7) | copy-start | bytes 3145732
  7.2 403.6 %all-gather.3.cloned.1.call-start = ((), (), s32[]{:S(2)}) async-start(), calls=%async_computation.1 | async-start | bytes 17825792 | tf_op jit(solution)/shard_map/all_gather | solution.py:52
  7.2 24.7 %collective-permute-start = (bf16[1,8,256,256]{3,2,1,0:T(8,128)(2,1)}, bf16[1,8,256,256]{3,2,1,0:T(8,128)(2,1)S(1)}, u32[]{:S(2)}, u32[]{:S(2)}) collective-permute-start(bf16[1,8,256,256]{3,2,1,0:T(8,128)(2,1)} %param.8), channel_id=1, source_target_pairs={{0,496},{16,0},{32,16},{48,32},{64,48},{80,64},{96,80},{112,96},{1... | collective-permute-start | bytes 3145736 | tf_op jit(solution)/shard_map/ppermute | solution.py:12
  24.5 3.5 copy-start.2
  58.5 540.4 %all-reduce.2.cloned.1.call-start = ((), (), s32[]{:S(2)}) async-start(), calls=%async_computation | async-start | bytes 1048576 | tf_op jit(solution)/shard_map/psum | solution.py:61
  410.8 7.0 %copy-start.1 = (bf16[1,4,256,256]{3,2,1,0:T(8,128)(2,1)S(1)}, bf16[1,4,256,256]{3,2,1,0:T(8,128)(2,1)}, u32[]{:S(2)}) copy-start(bf16[1,4,256,256]{3,2,1,0:T(8,128)(2,1)} %param.6) | copy-start | bytes 1572868
Sparse Core Ops, SparseCore 0:
  58.6 352.1 all-gather.2
  448.0 150.8 all-reduce.1
